TPU v7x, 32 devices: a whole 2x2x4 slice. The times are simulated.
32 devices in a mesh: trial: 4 (over z), row: 8 (over y, x, core).
Axes of the slice: x: 2, y: 2, z: 4, core: 2. Of those that a mesh axis runs over, the one named last changes fastest.
Arguments:
- phase_map: float32 [4096, 512], P('row'), may hold values from -3.140625 to 3.140625
- target: float32 [4096, 512], P('row'), may hold values from 0 to 2
- distance: float32 [4], P('trial'), may hold values from 0.25 to 1
- etch_class: int32 [4, 32, 4], P('trial', 'row'), may hold values from 0 to 3
- class_offset: float32 [4], replicated, may hold values from -0.6 to 0.6
- aperture_start: int32 [4], replicated, may hold values from 0 to 7
- aperture_stop: int32 [4], replicated, may hold values from 25 to 32
Outputs:
- phase_grad: float32 [4096, 512], P('row', 'trial')
Inputs may be any that keep to these rules, and one draw needn't show every extreme that they name: `etch_class`: etch bias classes.
All inputs are finite; a program needn't handle non-finite values.
Results may differ from a plain program's by a relative error of at most 0.02.
Values may be sent and summed in bfloat16 or wider, within the bound.
A program may use at most 64 MiB of HBM per device.

v0:
```python
import jax
import jax.numpy as jnp
from jax import lax
from jax.sharding import PartitionSpec as P

BLK = 128
HIGHEST_PRECISION = lax.Precision.HIGHEST


def cosine_pair(numer, denom):
    angle = -2.0 * jnp.pi / denom * numer.astype(jnp.float32)
    return (jnp.cos(angle), jnp.sin(angle))


def column_tables(width, kept):
    columns = jnp.arange(width, dtype=jnp.int32)
    freqs = jnp.arange(kept, dtype=jnp.int32) - kept // 2
    table_real, table_imag = cosine_pair(jnp.mod(columns[:, None] * freqs[None, :], width), width)
    table_real = table_real.astype(jnp.bfloat16)
    table_imag = table_imag.astype(jnp.bfloat16)
    forward = jnp.concatenate(
        [
            jnp.concatenate([table_real, table_imag], 1),
            jnp.concatenate([-table_imag, table_real], 1),
        ],
        0,
    )
    backward = jnp.concatenate(
        [
            jnp.concatenate([table_real.T, -table_imag.T], 1),
            jnp.concatenate([table_imag.T, table_real.T], 1),
        ],
        0,
    )
    return (forward, backward)


def block_tables(height):
    places = jnp.arange(height, dtype=jnp.int32)
    table_real, table_imag = cosine_pair(jnp.mod(places[:, None] * places[None, :], height), height)
    table_real = table_real.astype(jnp.bfloat16)
    table_imag = table_imag.astype(jnp.bfloat16)
    forward = jnp.concatenate(
        [
            jnp.concatenate([table_real, -table_imag], 1),
            jnp.concatenate([table_imag, table_real], 1),
        ],
        0,
    )
    backward = jnp.concatenate(
        [
            jnp.concatenate([table_real, table_imag], 1),
            jnp.concatenate([-table_imag, table_real], 1),
        ],
        0,
    )
    return (forward, backward)


def transfer_phase(signed, across, dist, global_rows, width):
    row_freq = signed.astype(jnp.float32)
    col_freq = across.astype(jnp.float32)
    theta = (
        -jnp.pi
        * dist
        * (
            row_freq * row_freq * (1.0 / global_rows)
            + col_freq * col_freq * (global_rows / (width * width))
        )
    )
    return (jnp.cos(theta), jnp.sin(theta))


def small_einsum(form, table, values):
    return jnp.einsum(form, table, values, precision=HIGHEST_PRECISION)


def local(phase_map, target, distance, etch_class, class_offset, aperture_start, aperture_stop):
    height, width = phase_map.shape
    kept = width // 2
    groups = lax.axis_size("row")
    device = lax.axis_index("row")
    global_rows = height * groups
    slim_cols = kept // groups
    col_fwd, col_back = column_tables(width, kept)
    blk_fwd, blk_back = block_tables(height)
    group_ids = jnp.arange(groups, dtype=jnp.int32)
    small_real, small_imag = cosine_pair(
        jnp.mod(group_ids[:, None] * group_ids[None, :], groups), groups
    )
    local_rows = jnp.arange(height, dtype=jnp.int32)
    dist = distance[0]
    classes = etch_class[0]
    row_blocks, col_blocks = classes.shape
    levels = jnp.arange(class_offset.shape[0], dtype=jnp.int32)
    offsets = jnp.sum(jnp.where(classes[:, :, None] == levels, class_offset, 0.0), axis=2)
    offset_map = jnp.broadcast_to(
        offsets[:, None, :, None], (row_blocks, BLK, col_blocks, BLK)
    ).reshape(height, width)
    row_block = (device * height + local_rows) // BLK
    first_block = jnp.broadcast_to(aperture_start[:, None], (col_blocks, BLK)).reshape(width)
    stop_block = jnp.broadcast_to(aperture_stop[:, None], (col_blocks, BLK)).reshape(width)
    inside = (row_block[:, None] >= first_block[None, :]) & (
        row_block[:, None] < stop_block[None, :]
    )
    aperture_mask = inside.astype(jnp.float32)
    angle_map = phase_map + offset_map
    lens_real = aperture_mask * jnp.cos(angle_map)
    lens_imag = aperture_mask * jnp.sin(angle_map)
    twist_cols_real, twist_cols_imag = cosine_pair(
        jnp.mod(group_ids[:, None] * local_rows[None, :], global_rows), global_rows
    )
    twist_cols_real = twist_cols_real[None]
    twist_cols_imag = twist_cols_imag[None]

    def forward_columns(cols_real, cols_imag):
        parts = (
            lax.all_to_all(cols_real, "row", split_axis=0, concat_axis=1, tiled=True),
            lax.all_to_all(cols_imag, "row", split_axis=0, concat_axis=1, tiled=True),
        )
        part_real = parts[0].reshape(slim_cols, groups, height).astype(jnp.float32)
        part_imag = parts[1].reshape(slim_cols, groups, height).astype(jnp.float32)
        mixed_real = small_einsum("kp,cpl->ckl", small_real, part_real) - small_einsum(
            "kp,cpl->ckl", small_imag, part_imag
        )
        mixed_imag = small_einsum("kp,cpl->ckl", small_real, part_imag) + small_einsum(
            "kp,cpl->ckl", small_imag, part_real
        )
        turned_real = (mixed_real * twist_cols_real - mixed_imag * twist_cols_imag).astype(
            jnp.bfloat16
        )
        turned_imag = (mixed_real * twist_cols_imag + mixed_imag * twist_cols_real).astype(
            jnp.bfloat16
        )
        stacked = jnp.concatenate([turned_real, turned_imag], 2)
        spectrum = jnp.einsum("ckl,ol->cko", stacked, blk_fwd, preferred_element_type=jnp.float32)
        return (spectrum[:, :, :height], spectrum[:, :, height:])

    def inverse_columns(filtered_real, filtered_imag):
        stacked = jnp.concatenate([filtered_real, filtered_imag], 2)
        unmixed = jnp.einsum("ckl,ol->cko", stacked, blk_back, preferred_element_type=jnp.float32)
        unmixed_real = unmixed[:, :, :height]
        unmixed_imag = unmixed[:, :, height:]
        returned_real = (
            (unmixed_real * twist_cols_real + unmixed_imag * twist_cols_imag)
            .astype(jnp.bfloat16)
            .astype(jnp.float32)
        )
        returned_imag = (
            (unmixed_imag * twist_cols_real - unmixed_real * twist_cols_imag)
            .astype(jnp.bfloat16)
            .astype(jnp.float32)
        )
        near_real = (
            small_einsum("kp,ckl->cpl", small_real, returned_real)
            + small_einsum("kp,ckl->cpl", small_imag, returned_imag)
        ) * (1.0 / global_rows)
        near_imag = (
            small_einsum("kp,ckl->cpl", small_real, returned_imag)
            - small_einsum("kp,ckl->cpl", small_imag, returned_real)
        ) * (1.0 / global_rows)
        near_real = near_real.astype(jnp.bfloat16).reshape(slim_cols, global_rows)
        near_imag = near_imag.astype(jnp.bfloat16).reshape(slim_cols, global_rows)
        owned = (
            lax.all_to_all(near_real, "row", split_axis=1, concat_axis=0, tiled=True),
            lax.all_to_all(near_imag, "row", split_axis=1, concat_axis=0, tiled=True),
        )
        return (owned[0], owned[1])

    freq_rows = group_ids[None, :, None] + groups * local_rows[None, None, :]
    across = (device * slim_cols + jnp.arange(slim_cols, dtype=jnp.int32) - kept // 2)[
        :, None, None
    ]
    signed = jnp.mod(freq_rows + global_rows // 2, global_rows) - global_rows // 2
    filter_real, filter_imag = transfer_phase(signed, across, dist, global_rows, width)

    def propagate(field_real, field_imag, phase_real, phase_imag):
        stacked_field = jnp.concatenate([field_real, field_imag], 1)
        flipped = jnp.einsum(
            "rc,cj->jr", stacked_field, col_fwd, preferred_element_type=jnp.float32
        ).astype(jnp.bfloat16)
        spec_real, spec_imag = forward_columns(flipped[:kept], flipped[kept:])
        filtered_real = (spec_real * phase_real - spec_imag * phase_imag).astype(jnp.bfloat16)
        filtered_imag = (spec_real * phase_imag + spec_imag * phase_real).astype(jnp.bfloat16)
        near_real, near_imag = inverse_columns(filtered_real, filtered_imag)
        result = jnp.einsum(
            "jr,jo->ro",
            jnp.concatenate([near_real, near_imag], 0),
            col_back,
            preferred_element_type=jnp.float32,
        ) * (1.0 / width)
        return (result[:, :width], result[:, width:])

    focal_real, focal_imag = propagate(
        lens_real.astype(jnp.bfloat16), lens_imag.astype(jnp.bfloat16), filter_real, filter_imag
    )
    residual = focal_real * focal_real + focal_imag * focal_imag - target
    back_real, back_imag = propagate(
        (residual * focal_real).astype(jnp.bfloat16),
        (residual * focal_imag).astype(jnp.bfloat16),
        filter_real,
        -filter_imag,
    )
    gradient = 2.0 * (lens_real * back_imag - lens_imag * back_real)
    return lax.psum_scatter(
        gradient.astype(jnp.bfloat16), "trial", scatter_dimension=1, tiled=True
    ).astype(jnp.float32)


def solution(mesh):
    return jax.shard_map(
        local,
        mesh=mesh,
        in_specs=(
            P("row", None),
            P("row", None),
            P("trial"),
            P("trial", "row", None),
            P(),
            P(),
            P(),
        ),
        out_specs=P("row", "trial"),
        check_vma=False,
    )
```

profile of v0, /device:TPU:0, one launch (start us, length us, event | category | flops | bytes accessed | tf_op | source)
XLA Modules:
  0.0 170.8 jit_solution(2126734685454798621)
XLA Ops:
  6.5 2.0 %fusion.99 = bf16[512,256]{1,0:T(8,128)(2,1)S(1)} fusion(s32[256]{0:T(256)S(1)} %iota_add_fusion.1), kind=kLoop, calls=%fused_computation.150 | loop fusion | flops 2359296 | bytes 263168 | tf_op jit(solution)/shard_map/neg | solution.py:24
  8.6 2.2 %sine_convert_fusion.2 = (bf16[512,256]{1,0:T(8,128)(2,1)S(1)}, bf16[512,256]{1,0:T(8,128)(2,1)S(1)}) fusion(s32[256]{0:T(256)S(1)} %iota_add_fusion.1), kind=kLoop, calls=%fused_computation.123 | loop fusion | flops 2097152 | bytes 525312 | tf_op jit(solution)/shard_map/convert_element_type | solution.py:20
  10.8 0.9 select_reduce_fusion
  11.8 0.7 broadcast_bitcast_fusion
  12.5 0.2 broadcast_in_dim.18
  12.7 4.2 %fusion.43 = (bf16[512,512]{1,0:T(8,128)(2,1)S(1)}, bf16[512,512]{1,0:T(8,128)(2,1)S(1)}) fusion(s32[512]{0:T(512)S(1)} %get-tuple-element.29, s32[512]{0:T(512)S(1)} %get-tuple-element.30, s32[512]{0:T(512)S(1)} %add_select_fusion.6, f32[512,512]{1,0:T(8,128)S(1)} %copy-done, f32[64,8,4,128]{3,2,1,0:T(4,128)S(1)} %bitcast.136), kind=kLoop, calls=%fused_computation.77 | loop fusion | flops 2097152 | bytes 3151872 | tf_op jit(solution)/shard_map/convert_element_type | solution.py:195
  17.0 0.8 convolution_convert_fusion.1
  17.7 0.8 fusion.234
  18.6 5.2 %all-to-all-start = ((bf16[8,32,512]{2,1,0:T(8,128)(2,1)}), bf16[8,32,512]{2,1,0:T(8,128)(2,1)S(1)}, u32[]{:S(2)}, u32[]{:S(2)}) async-start(bf16[8,32,512]{2,1,0:T(8,128)(2,1)} %bitcast.3), calls=%async_computation | async-start | bytes 524288 | tf_op jit(solution)/shard_map/all_to_all | solution.py:118
  23.9 4.6 %fusion.98 = bf16[512,512]{1,0:T(8,128)(2,1)} fusion(), kind=kLoop, calls=%fused_computation.149 | loop fusion | flops 4718592 | bytes 524288 | tf_op jit(solution)/shard_map/neg | solution.py:45
  28.5 4.6 %cosine_convert_fusion = bf16[512,512]{1,0:T(8,128)(2,1)} fusion(), kind=kLoop, calls=%fused_computation.64 | loop fusion | flops 3932160 | bytes 524288 | tf_op jit(solution)/shard_map/convert_element_type | solution.py:41
  33.1 4.6 %sine_convert_fusion = bf16[512,512]{1,0:T(8,128)(2,1)} fusion(), kind=kLoop, calls=%fused_computation.63 | loop fusion | flops 3932160 | bytes 524288 | tf_op jit(solution)/shard_map/convert_element_type | solution.py:42
  37.7 3.1 %sine_convert_fusion.1 = (bf16[256,512]{1,0:T(8,128)(2,1)S(1)}, bf16[256,512]{1,0:T(8,128)(2,1)}) fusion(s32[256]{0:T(256)S(1)} %iota_add_fusion.1), kind=kLoop, calls=%fused_computation.109 | loop fusion | flops 2097152 | bytes 525312 | tf_op jit(solution)/shard_map/convert_element_type | solution.py:20
  41.5 4.2 %all-to-all-start.1 = ((bf16[8,32,512]{2,1,0:T(8,128)(2,1)}), bf16[8,32,512]{2,1,0:T(8,128)(2,1)S(1)}, u32[]{:S(2)}, u32[]{:S(2)}) async-start(bf16[8,32,512]{2,1,0:T(8,128)(2,1)} %bitcast.6), calls=%async_computation.1 | async-start | bytes 524288 | tf_op jit(solution)/shard_map/all_to_all | solution.py:119
  45.7 0.5 fusion.88
  46.2 6.4 %all-to-all-done.1 = bf16[8,32,512]{2,1,0:T(8,128)(2,1)S(1)} async-done(((bf16[8,32,512]{2,1,0:T(8,128)(2,1)}), bf16[8,32,512]{2,1,0:T(8,128)(2,1)S(1)}, u32[]{:S(2)}, u32[]{:S(2)}) %all-to-all-start.1) | async-done | bytes 262176 | tf_op jit(solution)/shard_map/all_to_all | solution.py:119
  52.6 0.5 fusion.84
  53.1 0.5 fusion.15
  53.6 0.6 subtract_convert_fusion.5
  54.3 0.7 fusion.10
  55.0 2.3 %subtract_convert_fusion.4 = (bf16[32,8,512]{2,1,0:T(8,128)(2,1)S(1)}, bf16[32,8,512]{2,1,0:T(8,128)(2,1)S(1)}) fusion(f32[32,8,1024]{2,1,0:T(8,128)S(1)} %fusion.10, f32[32]{0:T(128)S(1)} %multiply_multiply_fusion, f32[8,512]{1,0:T(8,128)S(1)} %fusion.108, f32[]{:T(128)} %bitcast.14), kind=kLoop, calls=%fused_computation.116 | loop fusion | flops 1310720 | bytes 1589380 | tf_op jit(solution)/shard_map/convert_element_type | solution.py:183
  57.4 0.8 fusion.6
  58.1 0.2 add_convert_fusion.3
  58.3 0.4 fusion.133
  58.7 0.4 fusion.131
  59.1 0.4 fusion.24
  59.6 0.8 copy.58
  60.4 4.1 %all-to-all-start.2 = ((bf16[32,8,512]{2,0,1:T(8,128)(2,1)}), bf16[32,8,512]{2,0,1:T(8,128)(2,1)}, u32[]{:S(2)}, u32[]{:S(2)}) async-start(bf16[32,8,512]{2,0,1:T(8,128)(2,1)} %copy.58), calls=%async_computation.2 | async-start | bytes 524288 | tf_op jit(solution)/shard_map/all_to_all | solution.py:165
  64.4 0.4 fusion.25
  64.9 0.8 copy.59
  65.6 5.7 %all-to-all-done.2 = bf16[32,8,512]{2,0,1:T(8,128)(2,1)} async-done(((bf16[32,8,512]{2,0,1:T(8,128)(2,1)}), bf16[32,8,512]{2,0,1:T(8,128)(2,1)}, u32[]{:S(2)}, u32[]{:S(2)}) %all-to-all-start.2) | async-done | bytes 262176 | tf_op jit(solution)/shard_map/all_to_all | solution.py:165
  71.4 3.4 %all-to-all-start.3 = ((bf16[32,8,512]{2,0,1:T(8,128)(2,1)}), bf16[32,8,512]{2,0,1:T(8,128)(2,1)S(1)}, u32[]{:S(2)}, u32[]{:S(2)}) async-start(bf16[32,8,512]{2,0,1:T(8,128)(2,1)} %copy.59), calls=%async_computation.3 | async-start | bytes 524288 | tf_op jit(solution)/shard_map/all_to_all | solution.py:166
  74.8 2.2 %fusion.100 = bf16[256,512]{1,0:T(8,128)(2,1)S(1)} fusion(s32[256]{0:T(256)S(1)} %iota_add_fusion.1), kind=kLoop, calls=%fused_computation.151 | loop fusion | flops 2359296 | bytes 263168 | tf_op jit(solution)/shard_map/neg | solution.py:30
  77.0 4.7 %all-to-all-done.3 = bf16[32,8,512]{2,0,1:T(8,128)(2,1)S(1)} async-done(((bf16[32,8,512]{2,0,1:T(8,128)(2,1)}), bf16[32,8,512]{2,0,1:T(8,128)(2,1)S(1)}, u32[]{:S(2)}, u32[]{:S(2)}) %all-to-all-start.3) | async-done | bytes 262176 | tf_op jit(solution)/shard_map/all_to_all | solution.py:166
  81.6 1.8 %convolution_multiply_fusion.1 = f32[512,1024]{1,0:T(8,128)S(1)} fusion(bf16[256,512]{1,0:T(8,128)(2,1)S(1)} %bitcast.140, bf16[256,512]{1,0:T(8,128)(2,1)} %bitcast.20, bf16[256,512]{1,0:T(8,128)(2,1)S(1)} %copy-done.8, bf16[256,512]{1,0:T(8,128)(2,1)S(1)} %get-tuple-element.25, bf16[256,512]{1,0:T(8,128)(2,1)S(1)} %fusion.100), kind=kOutput, calls=%fused_computation.9 | convolution fusion | flops 542638080 | bytes 3407872 | tf_op jit(solution)/shard_map/jr,jo->ro/dot_general | solution.py:186
  83.4 0.4 multiply_convert_fusion.1
  83.9 0.5 copy-done.11
  84.5 0.8 convolution_convert_fusion
  85.3 0.7 fusion.233
  86.0 9.3 %all_to_all.128 = bf16[8,32,512]{2,1,0:T(8,128)(2,1)S(1)} all-to-all(bf16[8,32,512]{2,1,0:T(8,128)(2,1)S(1)} %bitcast.139), channel_id=1, replica_groups=mesh['trial'=4,'row'=8] {'row'}, dimensions={0} | all-to-all | bytes 524288 | tf_op jit(solution)/shard_map/all_to_all | solution.py:118
  95.3 3.6 %all-to-all-start.5 = ((bf16[8,32,512]{2,1,0:T(8,128)(2,1)}), bf16[8,32,512]{2,1,0:T(8,128)(2,1)S(1)}, u32[]{:S(2)}, u32[]{:S(2)}) async-start(bf16[8,32,512]{2,1,0:T(8,128)(2,1)} %bitcast.27), calls=%async_computation.5 | async-start | bytes 524288 | tf_op jit(solution)/shard_map/all_to_all | solution.py:119
  99.0 0.5 fusion.82
  99.5 6.1 %all-to-all-done.5 = bf16[8,32,512]{2,1,0:T(8,128)(2,1)S(1)} async-done(((bf16[8,32,512]{2,1,0:T(8,128)(2,1)}), bf16[8,32,512]{2,1,0:T(8,128)(2,1)S(1)}, u32[]{:S(2)}, u32[]{:S(2)}) %all-to-all-start.5) | async-done | bytes 262176 | tf_op jit(solution)/shard_map/all_to_all | solution.py:119
  105.6 0.5 fusion.78
  106.1 0.5 fusion.13
  106.6 0.6 subtract_convert_fusion.2
  107.3 0.8 fusion.8
  108.1 2.4 %subtract_convert_fusion.1 = (bf16[32,8,512]{2,1,0:T(8,128)(2,1)S(1)}, bf16[32,8,512]{2,1,0:T(8,128)(2,1)S(1)}) fusion(f32[32,8,1024]{2,1,0:T(8,128)S(1)} %fusion.8, f32[32]{0:T(128)S(1)} %multiply_multiply_fusion, f32[8,512]{1,0:T(8,128)S(1)} %fusion.108, f32[]{:T(128)} %bitcast.14), kind=kLoop, calls=%fused_computation.106 | loop fusion | flops 1441792 | bytes 1589380 | tf_op jit(solution)/shard_map/convert_element_type | solution.py:183
  110.4 0.8 fusion.4
  111.2 0.2 add_convert_fusion
  111.3 0.4 fusion.129
  111.8 0.4 fusion.127
  112.2 0.4 fusion.26
  112.6 0.8 copy.66
  113.4 4.0 %all-to-all-start.6 = ((bf16[32,8,512]{2,0,1:T(8,128)(2,1)}), bf16[32,8,512]{2,0,1:T(8,128)(2,1)}, u32[]{:S(2)}, u32[]{:S(2)}) async-start(bf16[32,8,512]{2,0,1:T(8,128)(2,1)} %copy.66), calls=%async_computation.6 | async-start | bytes 524288 | tf_op jit(solution)/shard_map/all_to_all | solution.py:165
  117.5 0.4 fusion.27
  118.0 6.3 %all-to-all-done.6 = bf16[32,8,512]{2,0,1:T(8,128)(2,1)} async-done(((bf16[32,8,512]{2,0,1:T(8,128)(2,1)}), bf16[32,8,512]{2,0,1:T(8,128)(2,1)}, u32[]{:S(2)}, u32[]{:S(2)}) %all-to-all-start.6) | async-done | bytes 262176 | tf_op jit(solution)/shard_map/all_to_all | solution.py:165
  124.4 9.3 %all_to_all.129 = bf16[32,8,512]{2,0,1:T(8,128)(2,1)S(1)} all-to-all(bf16[32,8,512]{2,0,1:T(8,128)(2,1)S(1)} %copy.67), channel_id=1, replica_groups=mesh['trial'=4,'row'=8] {'row'}, dimensions={1} | all-to-all | bytes 524288 | tf_op jit(solution)/shard_map/all_to_all | solution.py:166
  133.7 1.8 %convolution_multiply_fusion = f32[512,1024]{1,0:T(8,128)S(1)} fusion(bf16[256,512]{1,0:T(8,128)(2,1)S(1)} %bitcast.141, bf16[256,512]{1,0:T(8,128)(2,1)} %bitcast.36, bf16[256,512]{1,0:T(8,128)(2,1)S(1)} %copy-done.9, bf16[256,512]{1,0:T(8,128)(2,1)S(1)} %get-tuple-element.25, bf16[256,512]{1,0:T(8,128)(2,1)} %copy-done.16), kind=kOutput, calls=%fused_computation.8 | convolution fusion | flops 542638080 | bytes 3407872 | tf_op jit(solution)/shard_map/jr,jo->ro/dot_general | solution.py:186
  135.5 4.3 %fusion.33 = bf16[512,512]{1,0:T(8,128)(2,1)S(1)} fusion(f32[512,1024]{1,0:T(8,128)S(1)} %convolution_multiply_fusion, s32[512]{0:T(512)S(1)} %get-tuple-element.29, s32[512]{0:T(512)S(1)} %get-tuple-element.30, s32[512]{0:T(512)S(1)} %add_select_fusion.6, f32[512,512]{1,0:T(8,128)S(1)} %copy-done, f32[64,8,4,128]{3,2,1,0:T(4,128)S(1)} %bitcast.137), kind=kLoop, calls=%fused_computation.50 | loop fusion | flops 2883584 | bytes 4724736 | tf_op jit(solution)/shard_map/convert_element_type | solution.py:206
  139.8 1.0 copy.84
  140.9 21.4 %reduce-scatter.4.cloned.1.call-done = bf16[128,512]{1,0:T(8,128)(2,1)} async-done(((bf16[512,512]{1,0:T(8,128)(2,1)}), bf16[128,512]{1,0:T(8,128)(2,1)}) %reduce-scatter.4.cloned.1.call-update) | async-done | bytes 131088
  162.2 1.0 copy.85
  163.2 0.7 convert_element_type.296
  (43 shorter events, 0.5 us)
Async XLA Ops:
  6.5 6.2 %copy-start = (f32[512,512]{1,0:T(8,128)S(1)}, f32[512,512]{1,0:T(8,128)}, u32[]{:S(2)}) copy-start(f32[512,512]{1,0:T(8,128)} %param.7) | copy-start | bytes 3145732
  8.6 8.4 %copy-start.10 = (bf16[512,256]{1,0:T(8,128)(2,1)}, bf16[512,256]{1,0:T(8,128)(2,1)S(1)}, u32[]{:S(2)}) copy-start(bf16[512,256]{1,0:T(8,128)(2,1)S(1)} %fusion.99) | copy-start | bytes 786436
  10.8 6.2 %copy-start.12 = (bf16[512,256]{1,0:T(8,128)(2,1)}, bf16[512,256]{1,0:T(8,128)(2,1)S(1)}, u32[]{:S(2)}) copy-start(bf16[512,256]{1,0:T(8,128)(2,1)S(1)} %get-tuple-element.27) | copy-start | bytes 786436
  10.8 6.2 %copy-start.14 = (bf16[512,256]{1,0:T(8,128)(2,1)}, bf16[512,256]{1,0:T(8,128)(2,1)S(1)}, u32[]{:S(2)}) copy-start(bf16[512,256]{1,0:T(8,128)(2,1)S(1)} %get-tuple-element.28) | copy-start | bytes 786436
  18.6 22.9 %all-to-all-start = ((bf16[8,32,512]{2,1,0:T(8,128)(2,1)}), bf16[8,32,512]{2,1,0:T(8,128)(2,1)S(1)}, u32[]{:S(2)}, u32[]{:S(2)}) async-start(bf16[8,32,512]{2,1,0:T(8,128)(2,1)} %bitcast.3), calls=%async_computation | async-start | bytes 524288 | tf_op jit(solution)/shard_map/all_to_all | solution.py:118
  41.5 11.1 %all-to-all-start.1 = ((bf16[8,32,512]{2,1,0:T(8,128)(2,1)}), bf16[8,32,512]{2,1,0:T(8,128)(2,1)S(1)}, u32[]{:S(2)}, u32[]{:S(2)}) async-start(bf16[8,32,512]{2,1,0:T(8,128)(2,1)} %bitcast.6), calls=%async_computation.1 | async-start | bytes 524288 | tf_op jit(solution)/shard_map/all_to_all | solution.py:119
  52.6 1.7 copy-start.2
  52.6 1.7 copy-start.4
  52.6 1.7 copy-start.6
  59.1 22.5 %copy-start.8 = (bf16[256,512]{1,0:T(8,128)(2,1)S(1)}, bf16[256,512]{1,0:T(8,128)(2,1)}, u32[]{:S(2)}) copy-start(bf16[256,512]{1,0:T(8,128)(2,1)} %get-tuple-element.26) | copy-start | bytes 786436
  60.4 11.0 %all-to-all-start.2 = ((bf16[32,8,512]{2,0,1:T(8,128)(2,1)}), bf16[32,8,512]{2,0,1:T(8,128)(2,1)}, u32[]{:S(2)}, u32[]{:S(2)}) async-start(bf16[32,8,512]{2,0,1:T(8,128)(2,1)} %copy.58), calls=%async_computation.2 | async-start | bytes 524288 | tf_op jit(solution)/shard_map/all_to_all | solution.py:165
  71.4 10.3 %all-to-all-start.3 = ((bf16[32,8,512]{2,0,1:T(8,128)(2,1)}), bf16[32,8,512]{2,0,1:T(8,128)(2,1)S(1)}, u32[]{:S(2)}, u32[]{:S(2)}) async-start(bf16[32,8,512]{2,0,1:T(8,128)(2,1)} %copy.59), calls=%async_computation.3 | async-start | bytes 524288 | tf_op jit(solution)/shard_map/all_to_all | solution.py:166
  76.9 8.3 %copy-start.16 = (bf16[256,512]{1,0:T(8,128)(2,1)}, bf16[256,512]{1,0:T(8,128)(2,1)S(1)}, u32[]{:S(2)}) copy-start(bf16[256,512]{1,0:T(8,128)(2,1)S(1)} %fusion.100) | copy-start | bytes 786436
  81.6 1.8 %copy-start.1 = (f32[512,512]{1,0:T(8,128)S(1)}, f32[512,512]{1,0:T(8,128)}, u32[]{:S(2)}) copy-start(f32[512,512]{1,0:T(8,128)} %param.8) | copy-start | bytes 3145732
  83.4 1.0 copy-start.11
  83.4 1.0 copy-start.13
  83.4 1.1 copy-start.15
  95.3 10.3 %all-to-all-start.5 = ((bf16[8,32,512]{2,1,0:T(8,128)(2,1)}), bf16[8,32,512]{2,1,0:T(8,128)(2,1)S(1)}, u32[]{:S(2)}, u32[]{:S(2)}) async-start(bf16[8,32,512]{2,1,0:T(8,128)(2,1)} %bitcast.27), calls=%async_computation.5 | async-start | bytes 524288 | tf_op jit(solution)/shard_map/all_to_all | solution.py:119
  105.6 1.7 copy-start.3
  105.6 1.7 copy-start.5
  105.6 1.7 copy-start.7
  112.2 21.5 %copy-start.9 = (bf16[256,512]{1,0:T(8,128)(2,1)S(1)}, bf16[256,512]{1,0:T(8,128)(2,1)}, u32[]{:S(2)}) copy-start(bf16[256,512]{1,0:T(8,128)(2,1)} %get-tuple-element.26) | copy-start | bytes 786436
  113.4 11.0 %all-to-all-start.6 = ((bf16[32,8,512]{2,0,1:T(8,128)(2,1)}), bf16[32,8,512]{2,0,1:T(8,128)(2,1)}, u32[]{:S(2)}, u32[]{:S(2)}) async-start(bf16[32,8,512]{2,0,1:T(8,128)(2,1)} %copy.66), calls=%async_computation.6 | async-start | bytes 524288 | tf_op jit(solution)/shard_map/all_to_all | solution.py:165
  117.5 44.7 %reduce-scatter.4.cloned.1.call-start = ((), (), s32[]{:S(2)}) async-start(), calls=%async_computation.9 | async-start | bytes 655360
Sparse Core Ops, SparseCore 0:
  141.0 21.1 reduce-scatter.3
where the time goes:
time: 172 us; the launch traced here: 171 us
  waiting for transfers between devices  50.6 us (29%)
  other arithmetic  39.1 us (23%)
  starting transfers between devices  24.6 us (14%)
  blocking collectives  18.6 us (11%)
  matrix products  15.7 us (9%)
  between operations  14.6 us (8%)
  local copies, waits for them, and re-layouts  7.68 us (4%)
    unnamed x2, waiting for transfers between devices  21.4 us
    all_to_all x2, waiting for transfers between devices, forward_columns(): lax.all_to_all(cols_imag, 'row', split_axis=0, concat_axis=1, tiled=True)  12.5 us
    all_to_all x2, waiting for transfers between devices, inverse_columns(): lax.all_to_all(near_real, 'row', split_axis=1, concat_axis=0, tiled=True)  12.1 us
    all_to_all x1, blocking collectives, inverse_columns(): lax.all_to_all(near_imag, 'row', split_axis=1, concat_axis=0, tiled=True)  9.3 us
    all_to_all x1, blocking collectives, forward_columns(): lax.all_to_all(cols_real, 'row', split_axis=0, concat_axis=1, tiled=True)  9.3 us
    all_to_all x2, starting transfers between devices, inverse_columns(): lax.all_to_all(near_real, 'row', split_axis=1, concat_axis=0, tiled=True)  8.1 us
    all_to_all x2, starting transfers between devices, forward_columns(): lax.all_to_all(cols_imag, 'row', split_axis=0, concat_axis=1, tiled=True)  7.84 us
    dot_general x16, matrix products, small_einsum(): return jnp.einsum(form, table, values, precision=HIGHEST_PRECISION)  7.7 us
  transfers between devices with their start and end apart: 7, of which 6 were waited for; matrix products, arithmetic and copies ran while one was open for 13% of the time, Pallas kernels for 0%

commit v1 on v0

--- a/solution.py
+++ b/solution.py
@@ -5,6 +5,13 @@
 
 BLK = 128
 HIGHEST_PRECISION = lax.Precision.HIGHEST
+
+
+def stacked_exchange(array, axis, split, join):
+    peers = lax.axis_size(axis)
+    blocks = jnp.stack(jnp.split(array, peers, axis=split), axis=0)
+    blocks = lax.all_to_all(blocks, axis, split_axis=0, concat_axis=0)
+    return jnp.concatenate(blocks, axis=join)
 
 
 def cosine_pair(numer, denom):
@@ -163,7 +170,7 @@
         near_imag = near_imag.astype(jnp.bfloat16).reshape(slim_cols, global_rows)
         owned = (
             lax.all_to_all(near_real, "row", split_axis=1, concat_axis=0, tiled=True),
-            lax.all_to_all(near_imag, "row", split_axis=1, concat_axis=0, tiled=True),
+            stacked_exchange(near_imag, "row", 1, 0),
         )
         return (owned[0], owned[1])
 

time: 172 us -> 172 us (level)
  waiting for transfers between devices: 50.6 us -> 46.2 us
  local copies, waits for them, and re-layouts: 7.68 us -> 12 us
    unnamed x36 -> x52, local copies, waits for them, and re-layouts: 2.73 us -> 7.25 us
    all_to_all x2, waiting for transfers between devices: 12.1 us -> 7.7 us  [inverse_columns(): lax.all_to_all(near_real, 'row', split_axis=1, concat_axis=0, tiled=True)]
  transfers between devices with their start and end apart: 7 -> 7, of which waited for: 6 -> 6; matrix products, arithmetic and copies ran while one was open for 13% -> 15% of each run, Pallas kernels for 0% -> 0%
where the time goes in v1:
time: 172 us; the launch traced here: 171 us
  waiting for transfers between devices  46.2 us (27%)
  other arithmetic  39.1 us (23%)
  starting transfers between devices  24.6 us (14%)
  blocking collectives  18.6 us (11%)
  matrix products  15.7 us (9%)
  between operations  14.6 us (8%)
  local copies, waits for them, and re-layouts  12 us (7%)
    unnamed x2, waiting for transfers between devices  21.4 us
    all_to_all x2, waiting for transfers between devices, forward_columns(): lax.all_to_all(cols_imag, 'row', split_axis=0, concat_axis=1, tiled=True)  12.5 us
    all_to_all x1, blocking collectives, stacked_exchange(): blocks = lax.all_to_all(blocks, axis, split_axis=0, concat_axis=0)  9.3 us
    all_to_all x1, blocking collectives, forward_columns(): lax.all_to_all(cols_real, 'row', split_axis=0, concat_axis=1, tiled=True)  9.3 us
    all_to_all x2, starting transfers between devices, inverse_columns(): lax.all_to_all(near_real, 'row', split_axis=1, concat_axis=0, tiled=True)  8.1 us
    all_to_all x2, starting transfers between devices, forward_columns(): lax.all_to_all(cols_imag, 'row', split_axis=0, concat_axis=1, tiled=True)  7.84 us
    dot_general x16, matrix products, small_einsum(): return jnp.einsum(form, table, values, precision=HIGHEST_PRECISION)  7.7 us
    all_to_all x2, waiting for transfers between devices, inverse_columns(): lax.all_to_all(near_real, 'row', split_axis=1, concat_axis=0, tiled=True)  7.7 us
  transfers between devices with their start and end apart: 7, of which 6 were waited for; matrix products, arithmetic and copies ran while one was open for 15% of the time, Pallas kernels for 0%

profile of v1, /device:TPU:0, one launch (start us, length us, event | category | flops | bytes accessed | tf_op | source)
XLA Modules:
  0.0 170.8 jit_solution(8615563389585557649)
XLA Ops:
  6.5 2.0 %fusion.97 = bf16[512,256]{1,0:T(8,128)(2,1)S(1)} fusion(s32[256]{0:T(256)S(1)} %iota_add_fusion.1), kind=kLoop, calls=%fused_computation.148 | loop fusion | flops 2359296 | bytes 263168 | tf_op jit(solution)/shard_map/neg | solution.py:31
  8.6 2.2 %sine_convert_fusion.2 = (bf16[512,256]{1,0:T(8,128)(2,1)S(1)}, bf16[512,256]{1,0:T(8,128)(2,1)S(1)}) fusion(s32[256]{0:T(256)S(1)} %iota_add_fusion.1), kind=kLoop, calls=%fused_computation.121 | loop fusion | flops 2097152 | bytes 525312 | tf_op jit(solution)/shard_map/convert_element_type | solution.py:27
  10.8 0.9 select_reduce_fusion
  11.8 0.7 broadcast_bitcast_fusion
  12.7 4.2 %fusion.41 = (bf16[512,512]{1,0:T(8,128)(2,1)S(1)}, bf16[512,512]{1,0:T(8,128)(2,1)S(1)}) fusion(s32[512]{0:T(512)S(1)} %get-tuple-element.29, s32[512]{0:T(512)S(1)} %get-tuple-element.30, s32[512]{0:T(512)S(1)} %add_select_fusion.6, f32[512,512]{1,0:T(8,128)S(1)} %copy-done, f32[64,8,4,128]{3,2,1,0:T(4,128)S(1)} %bitcast.198), kind=kLoop, calls=%fused_computation.75 | loop fusion | flops 2097152 | bytes 3151872 | tf_op jit(solution)/shard_map/convert_element_type | solution.py:202
  17.0 0.8 convolution_convert_fusion.1
  17.7 0.8 fusion.232
  18.6 5.2 %all-to-all-start = ((bf16[8,32,512]{2,1,0:T(8,128)(2,1)}), bf16[8,32,512]{2,1,0:T(8,128)(2,1)S(1)}, u32[]{:S(2)}, u32[]{:S(2)}) async-start(bf16[8,32,512]{2,1,0:T(8,128)(2,1)} %bitcast.3), calls=%async_computation | async-start | bytes 524288 | tf_op jit(solution)/shard_map/all_to_all | solution.py:125
  23.9 4.6 %fusion.96 = bf16[512,512]{1,0:T(8,128)(2,1)} fusion(), kind=kLoop, calls=%fused_computation.147 | loop fusion | flops 4718592 | bytes 524288 | tf_op jit(solution)/shard_map/neg | solution.py:52
  28.5 4.6 %cosine_convert_fusion = bf16[512,512]{1,0:T(8,128)(2,1)} fusion(), kind=kLoop, calls=%fused_computation.62 | loop fusion | flops 3932160 | bytes 524288 | tf_op jit(solution)/shard_map/convert_element_type | solution.py:48
  33.1 4.6 %sine_convert_fusion = bf16[512,512]{1,0:T(8,128)(2,1)} fusion(), kind=kLoop, calls=%fused_computation.61 | loop fusion | flops 3932160 | bytes 524288 | tf_op jit(solution)/shard_map/convert_element_type | solution.py:49
  37.7 3.1 %sine_convert_fusion.1 = (bf16[256,512]{1,0:T(8,128)(2,1)S(1)}, bf16[256,512]{1,0:T(8,128)(2,1)}) fusion(s32[256]{0:T(256)S(1)} %iota_add_fusion.1), kind=kLoop, calls=%fused_computation.107 | loop fusion | flops 2097152 | bytes 525312 | tf_op jit(solution)/shard_map/convert_element_type | solution.py:27
  41.5 4.2 %all-to-all-start.1 = ((bf16[8,32,512]{2,1,0:T(8,128)(2,1)}), bf16[8,32,512]{2,1,0:T(8,128)(2,1)S(1)}, u32[]{:S(2)}, u32[]{:S(2)}) async-start(bf16[8,32,512]{2,1,0:T(8,128)(2,1)} %bitcast.6), calls=%async_computation.1 | async-start | bytes 524288 | tf_op jit(solution)/shard_map/all_to_all | solution.py:126
  45.7 0.5 fusion.86
  46.2 6.4 %all-to-all-done.1 = bf16[8,32,512]{2,1,0:T(8,128)(2,1)S(1)} async-done(((bf16[8,32,512]{2,1,0:T(8,128)(2,1)}), bf16[8,32,512]{2,1,0:T(8,128)(2,1)S(1)}, u32[]{:S(2)}, u32[]{:S(2)}) %all-to-all-start.1) | async-done | bytes 262176 | tf_op jit(solution)/shard_map/all_to_all | solution.py:126
  52.6 0.5 fusion.82
  53.1 0.5 fusion.15
  53.6 0.6 subtract_convert_fusion.5
  54.3 0.7 fusion.10
  55.0 2.3 %subtract_convert_fusion.4 = (bf16[32,8,512]{2,1,0:T(8,128)(2,1)S(1)}, bf16[32,8,512]{2,1,0:T(8,128)(2,1)S(1)}) fusion(f32[32,8,1024]{2,1,0:T(8,128)S(1)} %fusion.10, f32[32]{0:T(128)S(1)} %multiply_multiply_fusion, f32[8,512]{1,0:T(8,128)S(1)} %fusion.106, f32[]{:T(128)} %bitcast.14), kind=kLoop, calls=%fused_computation.114 | loop fusion | flops 1310720 | bytes 1589380 | tf_op jit(solution)/shard_map/convert_element_type | solution.py:190
  57.4 0.8 fusion.6
  59.1 0.4 fusion.24
  59.6 0.8 copy.54
  60.4 4.1 %all-to-all-start.2 = ((bf16[32,8,512]{2,0,1:T(8,128)(2,1)}), bf16[32,8,512]{2,0,1:T(8,128)(2,1)}, u32[]{:S(2)}, u32[]{:S(2)}) async-start(bf16[32,8,512]{2,0,1:T(8,128)(2,1)} %copy.54), calls=%async_computation.2 | async-start | bytes 524288 | tf_op jit(solution)/shard_map/all_to_all | solution.py:172
  64.4 0.4 fusion.22
  65.0 0.6 constant_dynamic-update-slice_fusion.7
  65.6 0.6 constant_dynamic-update-slice_fusion.6
  66.2 0.6 constant_dynamic-update-slice_fusion.5
  66.8 0.6 constant_dynamic-update-slice_fusion.4
  67.4 0.6 constant_dynamic-update-slice_fusion.3
  68.0 0.6 constant_dynamic-update-slice_fusion.2
  68.7 0.6 constant_dynamic-update-slice_fusion.1
  69.3 0.6 constant_dynamic-update-slice_fusion
  69.9 1.5 all-to-all-done.2
  71.4 3.4 %all-to-all-start.3 = ((bf16[8,32,512]{2,1,0:T(8,128)(2,1)}), bf16[8,32,512]{2,1,0:T(8,128)(2,1)S(1)}, u32[]{:S(2)}, u32[]{:S(2)}) async-start(bf16[8,32,512]{2,1,0:T(8,128)(2,1)} %constant_dynamic-update-slice_fusion), calls=%async_computation.3 | async-start | bytes 524288 | tf_op jit(solution)/shard_map/all_to_all | solution.py:13
  74.8 2.2 %fusion.98 = bf16[256,512]{1,0:T(8,128)(2,1)S(1)} fusion(s32[256]{0:T(256)S(1)} %iota_add_fusion.1), kind=kLoop, calls=%fused_computation.149 | loop fusion | flops 2359296 | bytes 263168 | tf_op jit(solution)/shard_map/neg | solution.py:37
  77.0 4.7 %all-to-all-done.3 = bf16[8,32,512]{2,1,0:T(8,128)(2,1)S(1)} async-done(((bf16[8,32,512]{2,1,0:T(8,128)(2,1)}), bf16[8,32,512]{2,1,0:T(8,128)(2,1)S(1)}, u32[]{:S(2)}, u32[]{:S(2)}) %all-to-all-start.3) | async-done | bytes 262176 | tf_op jit(solution)/shard_map/all_to_all | solution.py:13
  81.6 1.8 %convolution_multiply_fusion.1 = f32[512,1024]{1,0:T(8,128)S(1)} fusion(bf16[256,512]{1,0:T(8,128)(2,1)S(1)} %bitcast.220, bf16[256,512]{1,0:T(8,128)(2,1)} %bitcast.20, bf16[256,512]{1,0:T(8,128)(2,1)S(1)} %copy-done.8, bf16[256,512]{1,0:T(8,128)(2,1)S(1)} %get-tuple-element.25, bf16[256,512]{1,0:T(8,128)(2,1)S(1)} %fusion.98), kind=kOutput, calls=%fused_computation.9 | convolution fusion | flops 542638080 | bytes 3407872 | tf_op jit(solution)/shard_map/jr,jo->ro/dot_general | solution.py:193
  83.4 0.4 multiply_convert_fusion.1
  83.9 0.5 copy-done.11
  84.5 0.8 convolution_convert_fusion
  85.3 0.7 fusion.231
  86.0 9.3 %all_to_all.106 = bf16[8,32,512]{2,1,0:T(8,128)(2,1)S(1)} all-to-all(bf16[8,32,512]{2,1,0:T(8,128)(2,1)S(1)} %bitcast.217), channel_id=1, replica_groups=mesh['trial'=4,'row'=8] {'row'}, dimensions={0} | all-to-all | bytes 524288 | tf_op jit(solution)/shard_map/all_to_all | solution.py:125
  95.3 3.6 %all-to-all-start.5 = ((bf16[8,32,512]{2,1,0:T(8,128)(2,1)}), bf16[8,32,512]{2,1,0:T(8,128)(2,1)S(1)}, u32[]{:S(2)}, u32[]{:S(2)}) async-start(bf16[8,32,512]{2,1,0:T(8,128)(2,1)} %bitcast.34), calls=%async_computation.5 | async-start | bytes 524288 | tf_op jit(solution)/shard_map/all_to_all | solution.py:126
  99.0 0.5 fusion.80
  99.5 6.1 %all-to-all-done.5 = bf16[8,32,512]{2,1,0:T(8,128)(2,1)S(1)} async-done(((bf16[8,32,512]{2,1,0:T(8,128)(2,1)}), bf16[8,32,512]{2,1,0:T(8,128)(2,1)S(1)}, u32[]{:S(2)}, u32[]{:S(2)}) %all-to-all-start.5) | async-done | bytes 262176 | tf_op jit(solution)/shard_map/all_to_all | solution.py:126
  105.6 0.5 fusion.76
  106.1 0.5 fusion.13
  106.6 0.6 subtract_convert_fusion.2
  107.3 0.8 fusion.8
  108.1 2.4 %subtract_convert_fusion.1 = (bf16[32,8,512]{2,1,0:T(8,128)(2,1)S(1)}, bf16[32,8,512]{2,1,0:T(8,128)(2,1)S(1)}) fusion(f32[32,8,1024]{2,1,0:T(8,128)S(1)} %fusion.8, f32[32]{0:T(128)S(1)} %multiply_multiply_fusion, f32[8,512]{1,0:T(8,128)S(1)} %fusion.106, f32[]{:T(128)} %bitcast.14), kind=kLoop, calls=%fused_computation.104 | loop fusion | flops 1441792 | bytes 1589380 | tf_op jit(solution)/shard_map/convert_element_type | solution.py:190
  110.4 0.7 fusion.4
  112.2 0.4 fusion.25
  112.6 0.8 copy.61
  113.4 4.0 %all-to-all-start.6 = ((bf16[32,8,512]{2,0,1:T(8,128)(2,1)}), bf16[32,8,512]{2,0,1:T(8,128)(2,1)}, u32[]{:S(2)}, u32[]{:S(2)}) async-start(bf16[32,8,512]{2,0,1:T(8,128)(2,1)} %copy.61), calls=%async_computation.6 | async-start | bytes 524288 | tf_op jit(solution)/shard_map/all_to_all | solution.py:172
  117.5 0.4 fusion.20
  118.1 6.2 %all-to-all-done.6 = bf16[32,8,512]{2,0,1:T(8,128)(2,1)} async-done(((bf16[32,8,512]{2,0,1:T(8,128)(2,1)}), bf16[32,8,512]{2,0,1:T(8,128)(2,1)}, u32[]{:S(2)}, u32[]{:S(2)}) %all-to-all-start.6) | async-done | bytes 262176 | tf_op jit(solution)/shard_map/all_to_all | solution.py:172
  124.4 9.3 %all_to_all.107 = bf16[8,32,512]{2,1,0:T(8,128)(2,1)S(1)} all-to-all(bf16[8,32,512]{2,1,0:T(8,128)(2,1)S(1)} %constant_dynamic-update-slice_fusion.8), channel_id=1, replica_groups=mesh['trial'=4,'row'=8] {'row'}, dimensions={0} | all-to-all | bytes 524288 | tf_op jit(solution)/shard_map/all_to_all | solution.py:13
  133.7 1.8 %convolution_multiply_fusion = f32[512,1024]{1,0:T(8,128)S(1)} fusion(bf16[256,512]{1,0:T(8,128)(2,1)S(1)} %bitcast.221, bf16[256,512]{1,0:T(8,128)(2,1)} %bitcast.43, bf16[256,512]{1,0:T(8,128)(2,1)S(1)} %copy-done.9, bf16[256,512]{1,0:T(8,128)(2,1)S(1)} %get-tuple-element.25, bf16[256,512]{1,0:T(8,128)(2,1)} %copy-done.16), kind=kOutput, calls=%fused_computation.8 | convolution fusion | flops 542638080 | bytes 3407872 | tf_op jit(solution)/shard_map/jr,jo->ro/dot_general | solution.py:193
  135.5 4.3 %fusion.31 = bf16[512,512]{1,0:T(8,128)(2,1)S(1)} fusion(f32[512,1024]{1,0:T(8,128)S(1)} %convolution_multiply_fusion, s32[512]{0:T(512)S(1)} %get-tuple-element.29, s32[512]{0:T(512)S(1)} %get-tuple-element.30, s32[512]{0:T(512)S(1)} %add_select_fusion.6, f32[512,512]{1,0:T(8,128)S(1)} %copy-done, f32[64,8,4,128]{3,2,1,0:T(4,128)S(1)} %bitcast.199), kind=kLoop, calls=%fused_computation.48 | loop fusion | flops 2883584 | bytes 4724736 | tf_op jit(solution)/shard_map/convert_element_type | solution.py:213
  139.8 1.0 copy.78
  140.8 21.4 %reduce-scatter.4.cloned.1.call-done = bf16[128,512]{1,0:T(8,128)(2,1)} async-done(((bf16[512,512]{1,0:T(8,128)(2,1)}), bf16[128,512]{1,0:T(8,128)(2,1)}) %reduce-scatter.4.cloned.1.call-update) | async-done | bytes 131088
  162.2 1.0 copy.79
  163.2 0.7 convert_element_type.296
  (59 shorter events, 2.8 us)
Async XLA Ops:
  6.5 6.2 %copy-start = (f32[512,512]{1,0:T(8,128)S(1)}, f32[512,512]{1,0:T(8,128)}, u32[]{:S(2)}) copy-start(f32[512,512]{1,0:T(8,128)} %param.7) | copy-start | bytes 3145732
  8.6 8.4 %copy-start.10 = (bf16[512,256]{1,0:T(8,128)(2,1)}, bf16[512,256]{1,0:T(8,128)(2,1)S(1)}, u32[]{:S(2)}) copy-start(bf16[512,256]{1,0:T(8,128)(2,1)S(1)} %fusion.97) | copy-start | bytes 786436
  10.8 6.2 %copy-start.12 = (bf16[512,256]{1,0:T(8,128)(2,1)}, bf16[512,256]{1,0:T(8,128)(2,1)S(1)}, u32[]{:S(2)}) copy-start(bf16[512,256]{1,0:T(8,128)(2,1)S(1)} %get-tuple-element.27) | copy-start | bytes 786436
  10.8 6.2 %copy-start.14 = (bf16[512,256]{1,0:T(8,128)(2,1)}, bf16[512,256]{1,0:T(8,128)(2,1)S(1)}, u32[]{:S(2)}) copy-start(bf16[512,256]{1,0:T(8,128)(2,1)S(1)} %get-tuple-element.28) | copy-start | bytes 786436
  18.6 22.9 %all-to-all-start = ((bf16[8,32,512]{2,1,0:T(8,128)(2,1)}), bf16[8,32,512]{2,1,0:T(8,128)(2,1)S(1)}, u32[]{:S(2)}, u32[]{:S(2)}) async-start(bf16[8,32,512]{2,1,0:T(8,128)(2,1)} %bitcast.3), calls=%async_computation | async-start | bytes 524288 | tf_op jit(solution)/shard_map/all_to_all | solution.py:125
  41.5 11.1 %all-to-all-start.1 = ((bf16[8,32,512]{2,1,0:T(8,128)(2,1)}), bf16[8,32,512]{2,1,0:T(8,128)(2,1)S(1)}, u32[]{:S(2)}, u32[]{:S(2)}) async-start(bf16[8,32,512]{2,1,0:T(8,128)(2,1)} %bitcast.6), calls=%async_computation.1 | async-start | bytes 524288 | tf_op jit(solution)/shard_map/all_to_all | solution.py:126
  52.6 1.7 copy-start.2
  52.6 1.7 copy-start.4
  52.6 1.7 copy-start.6
  59.6 22.0 %copy-start.8 = (bf16[256,512]{1,0:T(8,128)(2,1)S(1)}, bf16[256,512]{1,0:T(8,128)(2,1)}, u32[]{:S(2)}) copy-start(bf16[256,512]{1,0:T(8,128)(2,1)} %get-tuple-element.26) | copy-start | bytes 786436
  60.4 11.0 %all-to-all-start.2 = ((bf16[32,8,512]{2,0,1:T(8,128)(2,1)}), bf16[32,8,512]{2,0,1:T(8,128)(2,1)}, u32[]{:S(2)}, u32[]{:S(2)}) async-start(bf16[32,8,512]{2,0,1:T(8,128)(2,1)} %copy.54), calls=%async_computation.2 | async-start | bytes 524288 | tf_op jit(solution)/shard_map/all_to_all | solution.py:172
  71.4 10.3 %all-to-all-start.3 = ((bf16[8,32,512]{2,1,0:T(8,128)(2,1)}), bf16[8,32,512]{2,1,0:T(8,128)(2,1)S(1)}, u32[]{:S(2)}, u32[]{:S(2)}) async-start(bf16[8,32,512]{2,1,0:T(8,128)(2,1)} %constant_dynamic-update-slice_fusion), calls=%async_computation.3 | async-start | bytes 524288 | tf_op jit(solution)/shard_map/all_to_all | solution.py:13
  76.9 8.3 %copy-start.16 = (bf16[256,512]{1,0:T(8,128)(2,1)}, bf16[256,512]{1,0:T(8,128)(2,1)S(1)}, u32[]{:S(2)}) copy-start(bf16[256,512]{1,0:T(8,128)(2,1)S(1)} %fusion.98) | copy-start | bytes 786436
  81.6 1.8 %copy-start.1 = (f32[512,512]{1,0:T(8,128)S(1)}, f32[512,512]{1,0:T(8,128)}, u32[]{:S(2)}) copy-start(f32[512,512]{1,0:T(8,128)} %param.8) | copy-start | bytes 3145732
  83.4 1.0 copy-start.11
  83.4 1.0 copy-start.13
  83.4 1.1 copy-start.15
  95.3 10.3 %all-to-all-start.5 = ((bf16[8,32,512]{2,1,0:T(8,128)(2,1)}), bf16[8,32,512]{2,1,0:T(8,128)(2,1)S(1)}, u32[]{:S(2)}, u32[]{:S(2)}) async-start(bf16[8,32,512]{2,1,0:T(8,128)(2,1)} %bitcast.34), calls=%async_computation.5 | async-start | bytes 524288 | tf_op jit(solution)/shard_map/all_to_all | solution.py:126
  105.6 1.7 copy-start.3
  105.6 1.7 copy-start.5
  105.6 1.7 copy-start.7
  112.6 21.1 %copy-start.9 = (bf16[256,512]{1,0:T(8,128)(2,1)S(1)}, bf16[256,512]{1,0:T(8,128)(2,1)}, u32[]{:S(2)}) copy-start(bf16[256,512]{1,0:T(8,128)(2,1)} %get-tuple-element.26) | copy-start | bytes 786436
  113.4 11.0 %all-to-all-start.6 = ((bf16[32,8,512]{2,0,1:T(8,128)(2,1)}), bf16[32,8,512]{2,0,1:T(8,128)(2,1)}, u32[]{:S(2)}, u32[]{:S(2)}) async-start(bf16[32,8,512]{2,0,1:T(8,128)(2,1)} %copy.61), calls=%async_computation.6 | async-start | bytes 524288 | tf_op jit(solution)/shard_map/all_to_all | solution.py:172
  117.5 44.7 %reduce-scatter.4.cloned.1.call-start = ((), (), s32[]{:S(2)}) async-start(), calls=%async_computation.9 | async-start | bytes 655360
Sparse Core Ops, SparseCore 0:
  141.0 21.1 reduce-scatter.3
